TPU v7x, 256 devices: a whole 4x4x8 slice. The times are simulated.
256 devices in a mesh: req: 16 (over z, core), mp: 16 (over x, y).
Axes of the slice: x: 4, y: 4, z: 8, core: 2. Of those that a mesh axis runs over, the one named last changes fastest.
Arguments:
- tokens: bfloat16 [1568, 7168], P('req', 'mp'), may hold values from -6 to 6
- layernorm_scale: float32 [7168], replicated, may hold values from 0.5 to 1.5
- layernorm_bias: float32 [7168], replicated, may hold values from -3 to 3
- query_key_value_weight: bfloat16 [3, 7168, 6144], P(None, 'req', 'mp'), may hold values from -0.0625 to 0.0625
- query_key_value_bias: float32 [3, 6144], P(None, 'mp'), may hold values from -3 to 3
- adapter_down_weight: bfloat16 [64, 7168, 32], P('req', 'mp'), may hold values from -0.0625 to 0.0625
- adapter_up_weight: bfloat16 [64, 2, 16, 6144], P('req', None, None, 'mp'), may hold values from -1.5 to 1.5
- adapter_index_table: int32 [16, 5], P('req'), may hold values from 0 to 63
- prompt_length_list: int32 [48], P('req'), may hold values from 1 to 32, 960 in all
- cache: bfloat16 [32, 2048, 2, 6144], P('req', None, None, 'mp'), may hold values from -320 to 320, as said below
- cache_length_list: int32 [32], P('req'), may hold values from 1 to 2048, 20480 in all
- output_weight: bfloat16 [6144, 7168], P('mp', 'req'), may hold values from -0.078125 to 0.078125
- output_bias: float32 [7168], P('mp'), may hold values from -3 to 3
Outputs:
- layer_out: bfloat16 [1568, 7168], P('req', 'mp')
Inputs may be any that keep to these rules, and one draw needn't show every extreme that they name: Each prompt fills the first prompt_length_list rows of its slot of 32 rows. Live cache positions are the first cache_length_list of each slot. `cache`: entries mostly of order one, though rare keys may be larger.
All inputs are finite; a program needn't handle non-finite values. No bound on the sum of `prompt_length_list` or of `cache_length_list` on one device may be relied on, other than what follows from the above.
Results may differ from a plain program's by a relative error of at most 0.015.
Values may be sent and summed in bfloat16 or wider, within the bound.
A program may use at most 128 MiB of HBM per device.

v0:
```python
import jax
import jax.numpy as jnp
from jax import lax
from jax.sharding import PartitionSpec as P

HEAD_DIM = 128
ADAPTER_RANK = 16


def layer_norm(row_data, gain_vec, shift_vec):
    values = row_data.astype(jnp.float32)
    average = jnp.mean(values, axis=-1, keepdims=True)
    centred = values - average
    variance = jnp.mean(centred * centred, axis=-1, keepdims=True)
    scaled = centred * lax.rsqrt(variance + 1e-05)
    return (scaled * gain_vec + shift_vec).astype(jnp.bfloat16)


def on_device(
    tokens,
    layernorm_scale,
    layernorm_bias,
    query_key_value_weight,
    query_key_value_bias,
    adapter_down_weight,
    adapter_up_weight,
    adapter_index_table,
    prompt_length_list,
    cache,
    cache_length_list,
    output_weight,
    output_bias,
):
    rows_dev = tokens.shape[0]
    part_cols = tokens.shape[1]
    decode_count = cache.shape[0]
    slot_count = prompt_length_list.shape[0]
    prompt_rows = rows_dev - decode_count
    slot_len = prompt_rows // slot_count
    rank_size = ADAPTER_RANK
    head_count = query_key_value_weight.shape[2] // HEAD_DIM
    score_scale = HEAD_DIM ** (-0.5)
    gathered = lax.all_gather(tokens, "mp", axis=1, tiled=True)
    normed = layer_norm(gathered, layernorm_scale, layernorm_bias)
    column = lax.axis_index("mp")
    slice_m = lax.dynamic_slice_in_dim(normed, column * part_cols, part_cols, 1)
    spread = lax.all_to_all(normed, "req", split_axis=1, concat_axis=0, tiled=True)
    projected = lax.psum_scatter(
        jnp.einsum(
            "rd,cde->rce", spread, query_key_value_weight, preferred_element_type=jnp.float32
        ),
        "req",
        scatter_dimension=0,
        tiled=True,
    )
    projected = projected + query_key_value_bias[None]
    positions = jnp.arange(rows_dev)
    request_slot = jnp.where(
        positions < prompt_rows, positions // slot_len, slot_count + positions - prompt_rows
    )
    slot_match = request_slot[:, None] == jnp.arange(slot_count + decode_count)[None, :]
    row_adapter = jnp.sum(jnp.where(slot_match, adapter_index_table[0][None, :], 0), axis=1)
    adapter_on_device = adapter_down_weight.shape[0]
    owners = lax.axis_size("req")
    owner_row = row_adapter // adapter_on_device
    to_owner = owner_row[None, :] == jnp.arange(owners)[:, None]
    outgoing = jnp.where(to_owner[:, :, None], slice_m[None], jnp.zeros((), jnp.bfloat16))
    labels = jnp.where(to_owner, (row_adapter - owner_row * adapter_on_device)[None, :], -1)
    received_rows = lax.all_to_all(outgoing, "req", split_axis=0, concat_axis=0, tiled=True)
    arrived_labels = lax.all_to_all(labels, "req", split_axis=0, concat_axis=0, tiled=True)
    sources, items = arrived_labels.shape
    selection_mask = (
        arrived_labels[:, :, None] == jnp.arange(adapter_on_device)[None, None, :]
    ).astype(jnp.float32)
    adapter_wise_sums = jnp.einsum(
        "yju,ouv->yjov", received_rows, adapter_down_weight, preferred_element_type=jnp.float32
    )
    reduced_rank_rows = jnp.einsum("ogf,ogft->ogt", selection_mask, adapter_wise_sums)
    reduced_rank_rows = lax.psum(reduced_rank_rows, "mp").astype(jnp.bfloat16)
    broadcast_rank_rows = selection_mask.astype(jnp.bfloat16)[
        :, :, :, None, None
    ] * reduced_rank_rows.reshape(sources, items, 1, 2, rank_size)
    corrections = jnp.einsum(
        "pqwgd,wgdx->pqgx",
        broadcast_rank_rows,
        adapter_up_weight,
        preferred_element_type=jnp.float32,
    ).astype(jnp.bfloat16)
    returned = lax.all_to_all(corrections, "req", split_axis=0, concat_axis=0, tiled=True)
    adapter_delta = jnp.sum(returned.astype(jnp.float32), axis=0)
    queries = (projected[:, 0] + adapter_delta[:, 0]).astype(jnp.bfloat16)
    keys_new = projected[:, 1].astype(jnp.bfloat16)
    values_new = (projected[:, 2] + adapter_delta[:, 1]).astype(jnp.bfloat16)
    prompt_q = queries[:prompt_rows].reshape(slot_count, slot_len, head_count, HEAD_DIM)
    prompt_k = keys_new[:prompt_rows].reshape(slot_count, slot_len, head_count, HEAD_DIM)
    prompt_v = values_new[:prompt_rows].reshape(slot_count, slot_len, head_count, HEAD_DIM)
    scores = (
        jnp.einsum("sihd,sjhd->shij", prompt_q, prompt_k, preferred_element_type=jnp.float32)
        * score_scale
    )
    causal = jnp.arange(slot_len)[None, :] <= jnp.arange(slot_len)[:, None]
    scores = jnp.where(causal[None, None], scores, -1e30)
    highest = jnp.max(scores, axis=3, keepdims=True)
    weights = jnp.where(causal[None, None], jnp.exp(scores - highest), 0.0)
    weights = (weights / jnp.sum(weights, axis=3, keepdims=True)).astype(jnp.bfloat16)
    prompt_out = jnp.einsum(
        "shij,sjhd->sihd", weights, prompt_v, preferred_element_type=jnp.float32
    )
    active = jnp.arange(slot_len)[None, :] < prompt_length_list[:, None]
    prompt_out = (
        jnp.where(active[:, :, None, None], prompt_out, 0.0)
        .astype(jnp.bfloat16)
        .reshape(prompt_rows, -1)
    )
    cache_len = cache.shape[1]
    decode_q = queries[prompt_rows:].reshape(decode_count, head_count, HEAD_DIM)
    decode_k = keys_new[prompt_rows:].reshape(decode_count, head_count, HEAD_DIM)
    decode_v = values_new[prompt_rows:].reshape(decode_count, head_count, HEAD_DIM)
    keys_old = cache[:, :, 0].reshape(decode_count, cache_len, head_count, HEAD_DIM)
    values_old = cache[:, :, 1].reshape(decode_count, cache_len, head_count, HEAD_DIM)
    cache_scores = (
        jnp.einsum("dhe,dthe->dht", decode_q, keys_old, preferred_element_type=jnp.float32)
        * score_scale
    )
    live_cache = jnp.arange(cache_len)[None, None, :] < cache_length_list[:, None, None]
    cache_scores = jnp.where(live_cache, cache_scores, -1e30)
    self_score = (
        jnp.einsum("dhe,dhe->dh", decode_q, decode_k, preferred_element_type=jnp.float32)
        * score_scale
    )
    row_top = jnp.maximum(jnp.max(cache_scores, axis=2), self_score)
    cache_weights = jnp.where(live_cache, jnp.exp(cache_scores - row_top[:, :, None]), 0.0)
    self_weight = jnp.exp(self_score - row_top)
    totals = jnp.sum(cache_weights, axis=2) + self_weight
    cache_weights = (cache_weights / totals[:, :, None]).astype(jnp.bfloat16)
    self_weight = (self_weight / totals).astype(jnp.bfloat16)
    decode_out = jnp.einsum(
        "dht,dthe->dhe", cache_weights, values_old, preferred_element_type=jnp.float32
    )
    decode_out = decode_out + self_weight.astype(jnp.float32)[:, :, None] * decode_v.astype(
        jnp.float32
    )
    decode_out = decode_out.astype(jnp.bfloat16).reshape(decode_count, -1)
    attended = jnp.concatenate([prompt_out, decode_out], axis=0)
    mixed = jnp.dot(
        attended,
        lax.all_gather(output_weight, "req", axis=1, tiled=True),
        preferred_element_type=jnp.float32,
    )
    summed = lax.psum_scatter(
        mixed.astype(jnp.bfloat16), "mp", scatter_dimension=1, tiled=True
    ).astype(jnp.float32)
    return (tokens.astype(jnp.float32) + summed + output_bias[None]).astype(jnp.bfloat16)


def solution(mesh):
    placed = (
        P("req", "mp"),
        P(),
        P(),
        P(None, "req", "mp"),
        P(None, "mp"),
        P("req", "mp", None),
        P("req", None, None, "mp"),
        P("req", None),
        P("req"),
        P("req", None, None, "mp"),
        P("req"),
        P("mp", "req"),
        P("mp"),
    )
    return jax.shard_map(
        on_device, mesh=mesh, in_specs=placed, out_specs=P("req", "mp"), check_vma=False
    )
```

profile of v0, /device:TPU:4, one launch (start us, length us, event | category | flops | bytes accessed | tf_op | source)
XLA Modules:
  0.0 484.9 jit_solution(15356733694840684768)
XLA Ops:
  6.5 0.7 all-gather.6.cloned.1.call-update
  7.3 0.0 all-reduce.4.cloned.1.call-start
  7.3 53.9 %all-gather.6.cloned.1.call-done = bf16[16,448,98]{1,2,0:T(8,128)(2,1)} async-done(((bf16[1,448,98]{1,2,0:T(8,128)(2,1)}), bf16[16,448,98]{1,2,0:T(8,128)(2,1)}) %all-gather.6.cloned.1.call-update) | async-done | bytes 1404944 | tf_op jit(solution)/shard_map/all_gather | solution.py:43
  61.2 3.6 copy.59
  64.8 4.7 reshape.248
  69.5 0.4 convert_reduce_fusion.1
  69.9 2.5 multiply_reduce_fusion
  72.4 1.7 fusion.1
  74.1 3.2 all_to_all.24
  77.3 0.9 copy.60
  78.2 49.3 %all_to_all.35 = bf16[98,16,448]{2,0,1:T(8,128)(2,1)S(1)} all-to-all(bf16[98,16,448]{2,0,1:T(8,128)(2,1)S(1)} %copy.60), channel_id=1, replica_groups=mesh['req'=16,'mp'=16] {'req'}, dimensions={1} | all-to-all | bytes 2809856 | tf_op jit(solution)/shard_map/all_to_all | solution.py:47
  127.5 1.7 all_to_all.27
  129.3 6.6 %fusion.5 = f32[1568,3,384]{2,0,1:T(8,128)} fusion(bf16[3,448,384]{2,1,0:T(8,128)(2,1)S(1)} %copy-done, bf16[1568,448]{1,0:T(8,128)(2,1)} %all_to_all.27), kind=kOutput, calls=%fused_computation.11 | convolution fusion | flops 1618477056 | bytes 9662464 | tf_op jit(solution)/shard_map/rd,cde->rce/dot_general | solution.py:49
  135.9 0.0 all-reduce.4.cloned.1.call-update
  136.0 0.6 copy-done.13
  136.6 0.1 select_reduce_fusion
  136.7 0.6 compare_select_fusion
  137.3 3.5 all-to-all-start.1
  140.8 1.0 constant_dynamic-slice_fusion.1
  141.8 1.5 broadcast_select_fusion
  143.3 4.9 %all-to-all-done.1 = s32[16,1,98]{2,1,0:T(1,128)S(1)} async-done(((s32[16,1,98]{2,1,0:T(1,128)}), s32[16,1,98]{2,1,0:T(1,128)S(1)}, u32[]{:S(2)}, u32[]{:S(2)}) %all-to-all-start.1) | async-done | bytes 6304 | tf_op jit(solution)/shard_map/all_to_all | solution.py:70
  148.2 3.7 all-to-all-start.2
  151.9 0.0 all-gather.4.cloned.1.call-start
  152.0 0.7 all-gather.4.cloned.1.call-update
  152.7 47.9 %all-to-all-done.2 = bf16[16,98,448]{2,1,0:T(8,128)(2,1)S(1)} async-done(((bf16[16,98,448]{2,1,0:T(8,128)(2,1)}), bf16[16,98,448]{2,1,0:T(8,128)(2,1)S(1)}, u32[]{:S(2)}, u32[]{:S(2)}) %all-to-all-start.2) | async-done | bytes 1404960 | tf_op jit(solution)/shard_map/all_to_all | solution.py:69
  200.6 0.8 fusion.10
  201.4 64.3 %all-reduce.5 = bf16[16,98,32]{1,2,0:T(8,128)(2,1)S(1)} all-reduce(f32[16,98,32]{1,2,0:T(8,128)S(1)} %fusion.10), channel_id=1, replica_groups=mesh['req'=16,'mp'=16] {'mp'}, use_global_device_ids=true, to_apply=%region_4.5 | all-reduce | flops 50176 | bytes 301056 | tf_op jit(solution)/shard_map/psum | solution.py:79
  265.7 0.9 fusion.2
  266.6 4.0 copy.65
  270.5 6.0 %all-to-all-start.3 = ((bf16[16,98,2,384]{3,2,1,0:T(2,128)(2,1)}), bf16[16,98,2,384]{3,2,1,0:T(2,128)(2,1)S(1)}, u32[]{:S(2)}, u32[]{:S(2)}) async-start(bf16[16,98,2,384]{3,2,1,0:T(2,128)(2,1)} %copy.65), calls=%async_computation.3 | async-start | bytes 4816896 | tf_op jit(solution)/shard_map/all_to_all | solution.py:89
  276.5 0.0 reduce-scatter.5.cloned.1.call-start
  276.6 13.8 %fusion.54 = (bf16[2,2048,1,384]{3,2,1,0:T(2,128)(2,1)}, bf16[2,2048,1,384]{3,2,1,0:T(2,128)(2,1)}) fusion(bf16[2,2048,2,384]{3,2,1,0:T(2,128)(2,1)} %param.22), kind=kLoop, calls=%fused_computation.103 | loop fusion | bytes 12582912 | tf_op jit(solution)/shard_map/slice | solution.py:119
  290.3 15.3 %copy.100 = bf16[2,2048,1,384]{1,3,0,2:T(8,128)(2,1)} copy(bf16[2,2048,1,384]{3,2,1,0:T(2,128)(2,1)} %get-tuple-element.9) | data formatting | bytes 6291456
  305.6 15.5 %copy.101 = bf16[2,2048,1,384]{1,3,0,2:T(8,128)(2,1)} copy(bf16[2,2048,1,384]{3,2,1,0:T(2,128)(2,1)} %get-tuple-element.10) | data formatting | bytes 6291456
  321.1 0.6 dynamic-slice
  322.4 0.1 iota_compare_fusion.5
  322.4 0.1 iota_compare_fusion.1
  322.5 23.7 %all-reduce.4.cloned.1.call-done = f32[1568,3,384]{2,0,1:T(8,128)} async-done(((f32[1568,3,384]{2,0,1:T(8,128)}), f32[1568,3,384]{2,0,1:T(8,128)}) %all-reduce.4.cloned.1.call-update) | async-done | bytes 7225360
  346.2 1.1 constant_dynamic-slice_fusion
  347.3 1.1 fusion.52
  348.4 0.4 slice_reduce_fusion
  348.9 2.0 convert_reduce_fusion
  350.9 0.3 fusion.22
  351.2 0.7 slice_reduce_fusion.1
  352.0 0.2 fusion.16
  352.2 0.1 fusion.55
  352.3 0.2 fusion.18
  352.5 0.1 copy.70
  352.6 0.1 fusion.41
  352.7 0.1 copy.89
  352.8 2.4 fusion.43
  355.2 0.1 fusion.38
  355.4 0.2 fusion.53
  355.6 0.1 copy.73
  355.8 0.1 fusion.37
  355.9 2.8 fusion.34
  358.7 0.1 fusion.45
  358.7 33.3 %all-gather.4.cloned.1.call-done = bf16[384,7168]{0,1:T(8,128)(2,1)} async-done(((bf16[384,448]{0,1:T(8,128)(2,1)}), bf16[384,7168]{0,1:T(8,128)(2,1)}) %all-gather.4.cloned.1.call-update) | async-done | bytes 5505040 | tf_op jit(solution)/shard_map/all_gather | solution.py:147
  392.1 5.0 %convolution_convert_fusion = bf16[98,7168]{1,0:T(8,128)(2,1)S(1)} fusion(bf16[384,7168]{0,1:T(8,128)(2,1)} %all-gather.4.cloned.1.call-done, bf16[2,384]{1,0:T(2,128)(2,1)S(1)} %bitcast.94, bf16[96,384]{1,0:T(8,128)(2,1)S(1)} %bitcast.91), kind=kOutput, calls=%fused_computation.1 | convolution fusion | flops 540345344 | bytes 6985216 | tf_op jit(solution)/shard_map/dot_general | solution.py:145
  397.1 2.4 copy.98
  399.5 0.0 reduce-scatter.5.cloned.1.call-update
  399.5 77.2 %reduce-scatter.5.cloned.1.call-done = bf16[448,98]{1,0:T(8,128)(2,1)} async-done(((bf16[7168,98]{1,0:T(8,128)(2,1)}), bf16[448,98]{1,0:T(8,128)(2,1)}) %reduce-scatter.5.cloned.1.call-update) | async-done | bytes 87824
  476.7 1.0 copy.99
  477.7 0.7 add_convert_fusion
  (53 shorter events, 0.4 us)
Async XLA Ops:
  6.5 122.7 %copy-start = (bf16[3,448,384]{2,1,0:T(8,128)(2,1)S(1)}, bf16[3,448,384]{2,1,0:T(8,128)(2,1)}, u32[]{:S(2)}) copy-start(bf16[3,448,384]{2,1,0:T(8,128)(2,1)} %param.16) | copy-start | bytes 3096580
  6.5 54.6 %all-gather.6.cloned.1.call-start = ((), (), s32[]{:S(2)}) async-start(), calls=%async_computation.6 | async-start | bytes 1810432 | tf_op jit(solution)/shard_map/all_gather | solution.py:43
  7.3 339.0 %all-reduce.4.cloned.1.call-start = ((), (), s32[]{:S(2)}) async-start(), calls=%async_computation.8 | async-start | bytes 14450688
  64.8 4.7 copy-start.3
  69.5 2.9 copy-start.2
  69.5 2.9 copy-start.7
  69.5 2.9 copy-start.8
  135.9 0.7 copy-start.13
  135.9 64.7 %copy-start.12 = (bf16[4,448,32]{1,2,0:T(8,128)(2,1)S(1)}, bf16[4,448,32]{1,2,0:T(8,128)(2,1)}, u32[]{:S(2)}) copy-start(bf16[4,448,32]{1,2,0:T(8,128)(2,1)} %param.18) | copy-start | bytes 344068
  137.3 10.9 %all-to-all-start.1 = ((s32[16,1,98]{2,1,0:T(1,128)}), s32[16,1,98]{2,1,0:T(1,128)S(1)}, u32[]{:S(2)}, u32[]{:S(2)}) async-start(s32[16,1,98]{2,1,0:T(1,128)} %compare_select_fusion), calls=%async_computation.1 | async-start | bytes 16384 | tf_op jit(solution)/shard_map/all_to_all | solution.py:70
  143.3 122.4 %copy-start.6 = (bf16[4,2,16,384]{3,2,1,0:T(8,128)(2,1)S(1)}, bf16[4,2,16,384]{3,2,1,0:T(8,128)(2,1)}, u32[]{:S(2)}) copy-start(bf16[4,2,16,384]{3,2,1,0:T(8,128)(2,1)} %param.19) | copy-start | bytes 294916
  148.2 52.4 %all-to-all-start.2 = ((bf16[16,98,448]{2,1,0:T(8,128)(2,1)}), bf16[16,98,448]{2,1,0:T(8,128)(2,1)S(1)}, u32[]{:S(2)}, u32[]{:S(2)}) async-start(bf16[16,98,448]{2,1,0:T(8,128)(2,1)} %broadcast_select_fusion), calls=%async_computation.2 | async-start | bytes 3407872 | tf_op jit(solution)/shard_map/all_to_all | solution.py:69
  151.9 240.2 %all-gather.4.cloned.1.call-start = ((), (), s32[]{:S(2)}) async-start(), calls=%async_computation.5 | async-start | bytes 5849088 | tf_op jit(solution)/shard_map/all_gather | solution.py:147
  270.5 78.4 %all-to-all-start.3 = ((bf16[16,98,2,384]{3,2,1,0:T(2,128)(2,1)}), bf16[16,98,2,384]{3,2,1,0:T(2,128)(2,1)S(1)}, u32[]{:S(2)}, u32[]{:S(2)}) async-start(bf16[16,98,2,384]{3,2,1,0:T(2,128)(2,1)} %copy.65), calls=%async_computation.3 | async-start | bytes 4816896 | tf_op jit(solution)/shard_map/all_to_all | solution.py:89
  276.5 200.2 %reduce-scatter.5.cloned.1.call-start = ((), (), s32[]{:S(2)}) async-start(), calls=%async_computation.7 | async-start | bytes 1949696
  305.6 15.5 %copy-start.15 = (u32[256]{0:T(256)S(1)}, u32[256]{0:T(256)}, u32[]{:S(2)}) copy-start(u32[256]{0:T(256)} %constant.76) | copy-start | bytes 3076
  305.6 16.7 %copy-start.14 = (s32[3]{0:T(128)S(1)}, s32[3]{0:T(128)}, u32[]{:S(2)}) copy-start(s32[3]{0:T(128)} %param.21) | copy-start | bytes 40
  305.6 16.8 %copy-start.11 = (s32[2]{0:T(128)S(1)}, s32[2]{0:T(128)}, u32[]{:S(2)}) copy-start(s32[2]{0:T(128)} %param.23) | copy-start | bytes 28
  305.6 41.7 %copy-start.9 = (f32[3,384]{1,0:T(4,128)S(1)}, f32[3,384]{1,0:T(4,128)}, u32[]{:S(2)}) copy-start(f32[3,384]{1,0:T(4,128)} %param.17) | copy-start | bytes 13828
  348.4 2.5 copy-start.4
  392.1 86.3 %copy-start.1 = (bf16[3,448,384]{2,1,0:T(8,128)(2,1)S(1)}, bf16[3,448,384]{2,1,0:T(8,128)(2,1)}, u32[]{:S(2)}) copy-start(bf16[3,448,384]{2,1,0:T(8,128)(2,1)} %param.16) | copy-start | bytes 3096580
  397.1 80.7 %copy-start.5 = (bf16[98,448]{1,0:T(8,128)(2,1)S(1)}, bf16[98,448]{1,0:T(8,128)(2,1)}, u32[]{:S(2)}) copy-start(bf16[98,448]{1,0:T(8,128)(2,1)} %param.13) | copy-start | bytes 263428
  397.1 80.6 %copy-start.10 = (f32[448]{0:T(512)S(1)}, f32[448]{0:T(512)}, u32[]{:S(2)}) copy-start(f32[448]{0:T(512)} %param.25) | copy-start | bytes 5380
Sparse Core Ops, SparseCore 0:
  9.8 51.3 all-gather.5
  136.1 210.1 all-reduce.3
  348.1 43.9 all-gather.3
  399.6 77.0 reduce-scatter.4
where the time goes:
time: 486 us; the launch traced here: 485 us
  waiting for transfers between devices  242 us (50%)
  blocking collectives  114 us (23%)
  local copies, waits for them, and re-layouts  71 us (15%)
  matrix products  18.9 us (4%)
  between operations  14.1 us (3%)
  starting transfers between devices  13.3 us (3%)
  other arithmetic  11.7 us (2%)
    unnamed x6, waiting for transfers between devices  102 us
    psum x1, blocking collectives, on_device(): reduced_rank_rows = lax.psum(reduced_rank_rows, 'mp').astype(jnp.bfloat16)  64.3 us
    all_gather x1, waiting for transfers between devices, on_device(): gathered = lax.all_gather(tokens, 'mp', axis=1, tiled=True)  53.9 us
    all_to_all x1, blocking collectives, on_device(): lax.all_to_all(normed, 'req', split_axis=1, concat_axis=0, tiled=True)  49.3 us
    all_to_all x1, waiting for transfers between devices, on_device(): lax.all_to_all(outgoing, 'req', split_axis=0, concat_axis=0, tiled=True)  47.9 us
    unnamed x40, local copies, waits for them, and re-layouts  36.5 us
    all_gather x1, waiting for transfers between devices, on_device(): lax.all_gather(output_weight, 'req', axis=1, tiled=True)  33.3 us
    slice x1, local copies, waits for them, and re-layouts, on_device(): cache[:, :, 0].reshape(decode_count, cache_len, head_count, HEAD_DIM)  13.8 us
  transfers between devices with their start and end apart: 7, of which 6 were waited for; matrix products, arithmetic and copies ran while one was open for 14% of the time, Pallas kernels for 0%

commit v1 on v0

v1 whole, which is shorter than its diff:
```python
import functools

import jax
import jax.numpy as jnp
from jax import lax
from jax.experimental import pallas as pl
from jax.experimental.pallas import tpu as pltpu
from jax.sharding import PartitionSpec as P

HEAD_DIM = 128
RANK = 16
NZ = 8
NM = 16
PAD = 112
MESH = pl.DeviceIdType.MESH
F32, BF16 = jnp.float32, jnp.bfloat16
VMEM_SPEC = pl.BlockSpec(memory_space=pltpu.VMEM)
SMEM_SPEC = pl.BlockSpec(memory_space=pltpu.SMEM)
ANY_SPEC = pl.BlockSpec(memory_space=pl.ANY)
LIMIT = 56 * 1024 * 1024


def place():
    r, m = lax.axis_index("req"), lax.axis_index("mp")
    return r // 2, r % 2, m


def at(z, c, m):
    return (z * 2 + c, m)


def signal(sem, device):
    pl.semaphore_signal(sem, inc=1, device_id=device, device_id_type=MESH)


def remote(src, dst, send, recv, device):
    return pltpu.make_async_remote_copy(
        src_ref=src, dst_ref=dst, send_sem=send, recv_sem=recv, device_id=device, device_id_type=MESH
    )


def plane_signal(barrier, z, c, m):
    def body(k, carry):
        signal(barrier, at(z, c, (m + k) % NM))
        return carry

    lax.fori_loop(1, NM, body, 0)


def ring_gather(z, c, m, out, send, recv):
    def step(way, s):
        sign = 1 - 2 * way
        block = (z + NZ - sign * s) % NZ
        target = at((z + NZ + sign) % NZ, c, m)
        return remote(out.at[block], out.at[block], send.at[way, s], recv.at[way, s], target)

    return step


def ring_steps():
    order = []
    for s in range(4):
        order.append((0, s))
        if s < 3:
            order.append((1, s))
    return order


def spread_kernel(
    tok, gains, w, wo, down, up,
    gathered, normed, w_both, wo_both, down_all, up_all,
    stats, tmp, mine, loc_sem, chip_send, chip_recv,
    st_send, st_recv, pm_send, pm_recv, ga_send, ga_recv,
    dn_send, dn_recv, up_send, up_recv, xd_send, xd_recv, xu_send, xu_recv,
):
    z, c, m = place()
    rows, cols = tok.shape
    other = at(z, 1 - c, m)
    tz, tm = m // 2, 2 * z + m % 2
    target = at(tz, c, tm)
    away = tz != z

    barrier = pltpu.get_barrier_semaphore()
    plane_signal(barrier, z, c, m)
    signal(barrier, other)
    signal(barrier, at((z + 1) % NZ, c, m))
    signal(barrier, at((z + NZ - 1) % NZ, c, m))

    @pl.when(away)
    def _():
        signal(barrier, target)

    x = tok[...].astype(F32)
    mean = jnp.sum(x, axis=1, keepdims=True) * (1.0 / cols)
    dev = x - mean
    m2 = jnp.sum(dev * dev, axis=1, keepdims=True)
    lane = lax.broadcasted_iota(jnp.int32, (rows, 128), 1)
    tmp[...] = jnp.zeros_like(tmp)
    tmp[0:rows, :] = jnp.where(lane == 0, mean, jnp.where(lane == 1, m2, 0.0))
    stats[m] = tmp[...].T[0:8, :]

    locals_ = [
        pltpu.make_async_copy(w, w_both.at[c], loc_sem.at[0]),
        pltpu.make_async_copy(wo, wo_both.at[c], loc_sem.at[1]),
        pltpu.make_async_copy(down, down_all.at[c, z], loc_sem.at[2]),
        pltpu.make_async_copy(up, up_all.at[c, z], loc_sem.at[3]),
    ]
    for one in locals_:
        one.start()

    pl.semaphore_wait(barrier, NM + 2 + jnp.minimum(jnp.abs(tz - z), 1))

    def stat(k):
        return remote(stats.at[m], stats.at[m], st_send.at[k], st_recv.at[k], at(z, c, (m + k) % NM))

    def start_stat(k, carry):
        stat(k).start()
        return carry

    lax.fori_loop(1, NM, start_stat, 0)

    locals_[2].wait()
    locals_[3].wait()
    dn_step = ring_gather(z, c, m, down_all.at[c], dn_send, dn_recv)
    up_step = ring_gather(z, c, m, up_all.at[c], up_send, up_recv)

    def cross(block, i):
        return (
            remote(down_all.at[c, block], down_all.at[c, block], xd_send.at[i], xd_recv.at[i], other),
            remote(up_all.at[c, block], up_all.at[c, block], xu_send.at[i], xu_recv.at[i], other),
        )

    for way in range(2):
        dn_step(way, 0).start()
        up_step(way, 0).start()
    for one in cross(z, 0):
        one.start()
    chip = [
        remote(w, w_both.at[c], chip_send.at[0], chip_recv.at[0], other),
        remote(wo, wo_both.at[c], chip_send.at[1], chip_recv.at[1], other),
    ]
    for one in chip:
        one.start()

    def wait_stat(k, carry):
        stat(k).wait()
        return carry

    lax.fori_loop(1, NM, wait_stat, 0)
    every = stats[...]
    means, m2s = every[:, 0, :], every[:, 1, :]
    mean = jnp.sum(means, axis=0, keepdims=True) * (1.0 / NM)
    off = means - mean
    total = jnp.sum(m2s, axis=0, keepdims=True) + cols * jnp.sum(off * off, axis=0, keepdims=True)
    inv = lax.rsqrt(total * (1.0 / (NM * cols)) + 1e-05)
    sub = lax.broadcasted_iota(jnp.int32, (128, 128), 0)
    tmp[...] = jnp.where(sub == 0, mean, jnp.where(sub == 1, inv, 0.0)).T
    both = tmp[0:rows, :]
    g = gains[...]
    value = (x - both[:, 0:1]) * both[:, 1:2] * g[0:1, :] + g[1:2, :]
    normed[...] = jnp.zeros_like(normed)
    normed[0:rows, :] = value.astype(BF16)

    perm = remote(normed, mine, pm_send, pm_recv, target)
    keep = pltpu.make_async_copy(normed, mine, loc_sem.at[4])

    @pl.when(away)
    def _():
        perm.start()
        perm.wait()

    @pl.when(jnp.logical_not(away))
    def _():
        keep.start()
        keep.wait()

    own = pltpu.make_async_copy(mine, gathered.at[m], loc_sem.at[5])
    own.start()

    def share(k):
        return remote(mine, gathered.at[m], ga_send.at[k], ga_recv.at[k], at(z, c, (m + k) % NM))

    def start_share(k, carry):
        share(k).start()
        return carry

    lax.fori_loop(1, NM, start_share, 0)

    i = 1
    for way, s in ring_steps():
        dn_step(way, s).wait()
        up_step(way, s).wait()
        sign = 1 - 2 * way
        if s + 1 < (4, 3)[way]:
            dn_step(way, s + 1).start()
            up_step(way, s + 1).start()
        for one in cross((z + NZ - sign * (s + 1)) % NZ, i):
            one.start()
        i += 1

    def wait_share(k, carry):
        share(k).wait()
        return carry

    lax.fori_loop(1, NM, wait_share, 0)
    own.wait()
    locals_[0].wait()
    locals_[1].wait()
    for one in chip:
        one.wait()
    for one in cross(z, 0):
        one.wait()
    i = 1
    for way, s in ring_steps():
        sign = 1 - 2 * way
        for one in cross((z + NZ - sign * (s + 1)) % NZ, i):
            one.wait()
        i += 1


def spread(tok, gains, w, wo, down, up):
    rows, cols = tok.shape
    dma = pltpu.SemaphoreType.DMA
    shape = jax.ShapeDtypeStruct
    return pl.pallas_call(
        spread_kernel,
        out_shape=(
            shape((NM, PAD, cols), BF16),
            shape((PAD, cols), BF16),
            shape((2, *w.shape), BF16),
            shape((2, *wo.shape), BF16),
            shape((2, NZ, *down.shape), BF16),
            shape((2, NZ, *up.shape), BF16),
        ),
        in_specs=[VMEM_SPEC, VMEM_SPEC, ANY_SPEC, ANY_SPEC, ANY_SPEC, ANY_SPEC],
        out_specs=(VMEM_SPEC, VMEM_SPEC, ANY_SPEC, ANY_SPEC, ANY_SPEC, ANY_SPEC),
        scratch_shapes=[
            pltpu.VMEM((NM, 8, 128), F32),
            pltpu.VMEM((128, 128), F32),
            pltpu.VMEM((PAD, cols), BF16),
            dma((6,)), dma((2,)), dma((2,)),
            dma((NM,)), dma((NM,)), dma, dma, dma((NM,)), dma((NM,)),
            dma((2, 4)), dma((2, 4)), dma((2, 4)), dma((2, 4)),
            dma((8,)), dma((8,)), dma((8,)), dma((8,)),
        ],
        compiler_params=pltpu.CompilerParams(collective_id=0, has_side_effects=True, vmem_limit_bytes=LIMIT),
        name="spread",
    )(tok, gains, w, wo, down, up)


def project_kernel(table, gathered, normed, w_both, down_all, part, low):
    cols = normed.shape[1]
    rows = PAD
    halves = [
        gathered[...].reshape(NZ, 2, rows, cols)[:, f].reshape(NZ * rows, cols) for f in range(2)
    ]
    for comp in range(3):
        acc = jnp.dot(halves[0], w_both[0, comp], preferred_element_type=F32)
        acc = acc + jnp.dot(halves[1], w_both[1, comp], preferred_element_type=F32)
        for h in range(3):
            part[:, comp * 3 + h] = acc[:, h * 128:(h + 1) * 128].reshape(NZ, rows, 128)
    slots = table.shape[1]
    per = down_all.shape[2]
    picked = []
    for s in range(slots):
        a = table[0, s]
        owner = a // per
        picked.append(down_all[owner % 2, owner // 2, a % per])
    stacked = jnp.concatenate(picked, axis=0)
    every = lax.dot_general(
        stacked, normed[...], (((1,), (1,)), ((), ())), preferred_element_type=F32
    )
    lane = lax.broadcasted_iota(jnp.int32, (2 * RANK, rows), 1)
    acc = jnp.zeros((2 * RANK, rows), F32)
    for s in range(slots):
        lo, hi = slot_rows(s)
        acc = jnp.where((lane >= lo) & (lane < hi), every[2 * RANK * s:2 * RANK * (s + 1)], acc)
    low[...] = jnp.zeros_like(low)
    low[:, 0:rows] = acc


def slot_rows(s):
    return (32 * s, 32 * s + 32) if s < 3 else (93 + s, 94 + s)


def project(table, gathered, normed, w_both, down_all):
    shape = jax.ShapeDtypeStruct
    return pl.pallas_call(
        project_kernel,
        out_shape=(shape((NZ, 9, PAD, 128), F32), shape((2 * RANK, 128), F32)),
        in_specs=[SMEM_SPEC, VMEM_SPEC, VMEM_SPEC, VMEM_SPEC, VMEM_SPEC],
        out_specs=(VMEM_SPEC, VMEM_SPEC),
        compiler_params=pltpu.CompilerParams(vmem_limit_bytes=LIMIT),
        name="project",
    )(table, gathered, normed, w_both, down_all)


def reduce_kernel(part, low, sums, lows, out_buf, in_buf, send, recv, lo_send, lo_recv, loc):
    z, c, m = place()
    barrier = pltpu.get_barrier_semaphore()
    plane_signal(barrier, z, c, m)
    signal(barrier, at((z + 1) % NZ, c, m))
    signal(barrier, at((z + NZ - 1) % NZ, c, m))
    pl.semaphore_wait(barrier, NM + 1)

    def ways():
        return [1] * 4 + [1 - 2 * c] + [-1] * 4

    def hop(j, way, s):
        return remote(
            out_buf.at[s, j], in_buf.at[s, j], send.at[s, j], recv.at[s, j], at((z + NZ + way) % NZ, c, m)
        )

    for j, way in enumerate(ways()):
        out_buf[0, j] = part[(z + NZ - way) % NZ, j].astype(BF16)
        hop(j, way, 0).start()

    def give(k):
        return remote(low, lows.at[m], lo_send.at[k], lo_recv.at[k], at(z, c, (m + k) % NM))

    def start_give(k, carry):
        give(k).start()
        return carry

    lax.fori_loop(1, NM, start_give, 0)
    own = pltpu.make_async_copy(low, lows.at[m], loc)
    own.start()

    def step(s, carry):
        for j, way in enumerate(ways()):
            hop(j, way, s - 1).wait_recv()
            block = (z + 2 * NZ - way * (1 + s)) % NZ
            out_buf[s, j] = (in_buf[s - 1, j].astype(F32) + part[block, j]).astype(BF16)
            hop(j, way, s).start()
        return carry

    lax.fori_loop(1, NZ - 1, step, 0)
    for j, way in enumerate(ways()):
        hop(j, way, NZ - 2).wait_recv()
        sums[j] = in_buf[NZ - 2, j].astype(F32) + part[z, j]

    def finish(s, carry):
        for j, way in enumerate(ways()):
            hop(j, way, s).wait_send()
        return carry

    lax.fori_loop(0, NZ - 1, finish, 0)

    def wait_give(k, carry):
        give(k).wait()
        return carry

    lax.fori_loop(1, NM, wait_give, 0)
    own.wait()


def reduce(part, low):
    dma = pltpu.SemaphoreType.DMA
    shape = jax.ShapeDtypeStruct
    return pl.pallas_call(
        reduce_kernel,
        out_shape=(shape((9, PAD, 128), F32), shape((NM, 2 * RANK, 128), F32)),
        in_specs=[VMEM_SPEC, VMEM_SPEC],
        out_specs=(VMEM_SPEC, VMEM_SPEC),
        scratch_shapes=[
            pltpu.VMEM((NZ - 1, 9, PAD, 128), BF16),
            pltpu.VMEM((NZ - 1, 9, PAD, 128), BF16),
            dma((NZ - 1, 9)), dma((NZ - 1, 9)), dma((NM,)), dma((NM,)), dma,
        ],
        compiler_params=pltpu.CompilerParams(collective_id=1, has_side_effects=True, vmem_limit_bytes=LIMIT),
        name="reduce",
    )(part, low)


def attend_kernel(table, lengths, cache_lengths, sums, lows, up_all, bias, cache, out, q_bd):
    rows = PAD
    scale = HEAD_DIM ** (-0.5)
    low = jnp.sum(lows[...], axis=0)[:, 0:rows].astype(BF16)
    slots = table.shape[1]
    per = up_all.shape[2]
    lane = lax.broadcasted_iota(jnp.int32, (RANK, rows), 1)
    deltas = []
    for which in range(2):
        left, right = [], []
        half = low[RANK * which:RANK * (which + 1)]
        for s in range(slots):
            lo, hi = slot_rows(s)
            left.append(jnp.where((lane >= lo) & (lane < hi), half, jnp.zeros((), BF16)))
            a = table[0, s]
            owner = a // per
            right.append(up_all[owner % 2, owner // 2, a % per, which])
        deltas.append(
            lax.dot_general(
                jnp.concatenate(left, axis=0), jnp.concatenate(right, axis=0),
                (((0,), (0,)), ((), ())), preferred_element_type=F32,
            ).astype(BF16).astype(F32)
        )
    ri = lax.broadcasted_iota(jnp.int32, (rows, rows), 0)
    ci = lax.broadcasted_iota(jnp.int32, (rows, rows), 1)
    seen = (ri // 32 == ci // 32) & (ci <= ri)
    row = lax.broadcasted_iota(jnp.int32, (rows, 1), 0)
    live = jnp.zeros((rows, 1), jnp.bool_)
    for s in range(3):
        live = live | ((row >= 32 * s) & (row < 32 * s + lengths[s]))
    qs, ks, vs = [], [], []
    for h in range(3):
        cut = slice(h * 128, (h + 1) * 128)
        qs.append((sums[h] + bias[h] + deltas[0][:, cut]).astype(BF16))
        ks.append((sums[3 + h] + bias[3 + h]).astype(BF16))
        vs.append((sums[6 + h] + bias[6 + h] + deltas[1][:, cut]).astype(BF16))
    span = cache.shape[1]
    q_bd[...] = jnp.zeros_like(q_bd)
    prompt = []
    for h in range(3):
        s = lax.dot_general(qs[h], ks[h], (((1,), (1,)), ((), ())), preferred_element_type=F32) * scale
        s = jnp.where(seen, s, -1e30)
        e = jnp.where(seen, jnp.exp(s - jnp.max(s, axis=1, keepdims=True)), 0.0)
        p = (e / jnp.sum(e, axis=1, keepdims=True)).astype(BF16)
        o = jnp.dot(p, vs[h], preferred_element_type=F32)
        prompt.append(jnp.where(live, o, 0.0))
    pos = lax.broadcasted_iota(jnp.int32, (8, span), 1)
    for d in range(2):
        n = 96 + d
        kv = cache[d]
        self_s = []
        for h in range(3):
            q_bd[h:h + 1, h * 128:(h + 1) * 128] = qs[h][n:n + 1].astype(F32)
            self_s.append(
                jnp.sum(qs[h][n:n + 1].astype(F32) * ks[h][n:n + 1].astype(F32), axis=1, keepdims=True)
            )
        own = jnp.concatenate(self_s + [jnp.zeros((5, 1), F32)], axis=0) * scale
        s = lax.dot_general(
            q_bd[...].astype(BF16), kv, (((1,), (1,)), ((), ())), preferred_element_type=F32
        ) * scale
        ok = (pos % 2 == 0) & (pos < 2 * cache_lengths[d])
        s = jnp.where(ok, s, -1e30)
        top = jnp.maximum(jnp.max(s, axis=1, keepdims=True), own)
        e = jnp.where(ok, jnp.exp(s - top), 0.0)
        mine = jnp.exp(own - top)
        total = jnp.sum(e, axis=1, keepdims=True) + mine
        p = pltpu.roll(e / total, 1, 1).astype(BF16)
        mine = (mine / total).astype(BF16).astype(F32)
        o = jnp.dot(p, kv, preferred_element_type=F32)
        for h in range(3):
            got = o[h:h + 1, h * 128:(h + 1) * 128] + mine[h:h + 1] * vs[h][n:n + 1].astype(F32)
            prompt[h] = jnp.where(row == n, got, prompt[h])
    for h in range(3):
        out[:, h * 128:(h + 1) * 128] = prompt[h].astype(BF16)


def attend(table, lengths, cache_lengths, sums, lows, up_all, bias, cache):
    return pl.pallas_call(
        attend_kernel,
        out_shape=jax.ShapeDtypeStruct((PAD, 384), BF16),
        in_specs=[SMEM_SPEC] * 3 + [VMEM_SPEC] * 5,
        out_specs=VMEM_SPEC,
        scratch_shapes=[pltpu.VMEM((8, 384), F32)],
        compiler_params=pltpu.CompilerParams(vmem_limit_bytes=LIMIT),
        name="attend",
    )(table, lengths, cache_lengths, sums, lows, up_all, bias, cache)


def collect_kernel(att, every, loc, send, recv):
    z, c, m = place()
    barrier = pltpu.get_barrier_semaphore()
    signal(barrier, at((z + 1) % NZ, c, m))
    signal(barrier, at((z + NZ - 1) % NZ, c, m))
    own = pltpu.make_async_copy(att, every.at[z], loc)
    own.start()
    own.wait()
    pl.semaphore_wait(barrier, 2)
    hop = ring_gather(z, c, m, every, send, recv)
    for way in range(2):
        hop(way, 0).start()
    for way, s in ring_steps():
        hop(way, s).wait()
        if s + 1 < (4, 3)[way]:
            hop(way, s + 1).start()


def collect(att):
    dma = pltpu.SemaphoreType.DMA
    return pl.pallas_call(
        collect_kernel,
        out_shape=jax.ShapeDtypeStruct((NZ, *att.shape), BF16),
        in_specs=[VMEM_SPEC],
        out_specs=VMEM_SPEC,
        scratch_shapes=[dma, dma((2, 4)), dma((2, 4))],
        compiler_params=pltpu.CompilerParams(collective_id=2, has_side_effects=True, vmem_limit_bytes=LIMIT),
        name="collect",
    )(att)


def mix_kernel(every, wo_both, out):
    a = every[...].reshape(NZ * PAD, every.shape[2])
    for f in range(2):
        o = lax.dot_general(a, wo_both[f], (((1,), (1,)), ((), ())), preferred_element_type=F32)
        o = o.astype(BF16).reshape(NZ, PAD, o.shape[1])
        for d in range(NZ):
            out[2 * d + f] = o[d]


def mix(every, wo_both):
    return pl.pallas_call(
        mix_kernel,
        out_shape=jax.ShapeDtypeStruct((NM, PAD, wo_both.shape[1]), BF16),
        in_specs=[VMEM_SPEC] * 2,
        out_specs=VMEM_SPEC,
        compiler_params=pltpu.CompilerParams(vmem_limit_bytes=LIMIT),
        name="mix",
    )(every, wo_both)


def scatter_kernel(pieces, tok, bias, out, came, total, back, loc, send, recv, pm_send, pm_recv):
    z, c, m = place()
    tz, tm = m // 2, 2 * z + m % 2
    target = at(tz, c, tm)
    away = tz != z
    rows = tok.shape[0]
    barrier = pltpu.get_barrier_semaphore()
    plane_signal(barrier, z, c, m)

    @pl.when(away)
    def _():
        signal(barrier, target)

    pl.semaphore_wait(barrier, NM - 1 + jnp.minimum(jnp.abs(tz - z), 1))

    def give(k):
        to = (m + k) % NM
        return remote(pieces.at[to], came.at[k], send.at[k], recv.at[k], at(z, c, to))

    def start(k, carry):
        give(k).start()
        return carry

    lax.fori_loop(1, NM, start, 0)
    total[...] = pieces[m].astype(F32)

    def add(k, carry):
        give(k).wait()
        total[...] += came[k].astype(F32)
        return carry

    lax.fori_loop(1, NM, add, 0)
    perm = remote(total, back, pm_send, pm_recv, target)
    keep = pltpu.make_async_copy(total, back, loc)

    @pl.when(away)
    def _():
        perm.start()
        perm.wait()

    @pl.when(jnp.logical_not(away))
    def _():
        keep.start()
        keep.wait()

    out[...] = (tok[...].astype(F32) + back[0:rows, :] + bias[...]).astype(BF16)


def scatter(pieces, tok, bias):
    dma = pltpu.SemaphoreType.DMA
    return pl.pallas_call(
        scatter_kernel,
        out_shape=jax.ShapeDtypeStruct(tok.shape, BF16),
        in_specs=[VMEM_SPEC] * 3,
        out_specs=VMEM_SPEC,
        scratch_shapes=[
            pltpu.VMEM(pieces.shape, BF16),
            pltpu.VMEM(pieces.shape[1:], F32),
            pltpu.VMEM(pieces.shape[1:], F32),
            dma, dma((NM,)), dma((NM,)), dma, dma,
        ],
        compiler_params=pltpu.CompilerParams(collective_id=3, has_side_effects=True, vmem_limit_bytes=LIMIT),
        name="scatter",
    )(pieces, tok, bias)


def on_device(
    tokens,
    layernorm_scale,
    layernorm_bias,
    query_key_value_weight,
    query_key_value_bias,
    adapter_down_weight,
    adapter_up_weight,
    adapter_index_table,
    prompt_length_list,
    cache,
    cache_length_list,
    output_weight,
    output_bias,
):
    cols = tokens.shape[1]
    m = lax.axis_index("mp")
    gains = jnp.stack(
        [lax.dynamic_slice_in_dim(v, m * cols, cols, 0) for v in (layernorm_scale, layernorm_bias)]
    )
    gathered, normed, w_both, wo_both, down_all, up_all = spread(
        tokens, gains, query_key_value_weight, output_weight.T,
        adapter_down_weight.transpose(0, 2, 1), adapter_up_weight,
    )
    part, low = project(adapter_index_table, gathered, normed, w_both, down_all)
    sums, lows = reduce(part, low)
    bias = query_key_value_bias.reshape(9, 1, 128)
    att = attend(
        adapter_index_table, prompt_length_list, cache_length_list, sums, lows, up_all, bias,
        cache.reshape(2, cache.shape[1] * 2, cache.shape[3]),
    )
    every = collect(att)
    pieces = mix(every, wo_both)
    return scatter(pieces, tokens, output_bias[None])


def solution(mesh):
    placed = (
        P("req", "mp"),
        P(),
        P(),
        P(None, "req", "mp"),
        P(None, "mp"),
        P("req", "mp", None),
        P("req", None, None, "mp"),
        P("req", None),
        P("req"),
        P("req", None, None, "mp"),
        P("req"),
        P("mp", "req"),
        P("mp"),
    )
    return jax.shard_map(
        on_device, mesh=mesh, in_specs=placed, out_specs=P("req", "mp"), check_vma=False
    )
```

time: 486 us -> 248 us (0.51)
  the two profiles are of different devices: /device:TPU:4 before, /device:TPU:42 now
where the time goes in v1:
time: 248 us; the launch traced here: 247 us
  Pallas kernels  229 us (92%)
  local copies, waits for them, and re-layouts  17.4 us (7%)
    pallas_call x1, Pallas kernels, spread(): pl.pallas_call(spread_kernel, out_shape=(shape((NM, PAD, cols), BF16), sh...  94.7 us
    pallas_call x1, Pallas kernels, scatter(): pl.pallas_call(scatter_kernel, out_shape=jax.ShapeDtypeStruct(tok.shape,...  52.6 us
    pallas_call x1, Pallas kernels, reduce(): pl.pallas_call(reduce_kernel, out_shape=(shape((9, PAD, 128), F32), shape...  44 us
    pallas_call x1, Pallas kernels, collect(): pl.pallas_call(collect_kernel, out_shape=jax.ShapeDtypeStruct((NZ, *att.s...  17.9 us
    reshape x1, local copies, waits for them, and re-layouts, on_device(): cache.reshape(2, cache.shape[1] * 2, cache.shape[3])  13.7 us
    pallas_call x1, Pallas kernels, attend(): pl.pallas_call(attend_kernel, out_shape=jax.ShapeDtypeStruct((PAD, 384),...  8.37 us
    pallas_call x1, Pallas kernels, project(): pl.pallas_call(project_kernel, out_shape=(shape((NZ, 9, PAD, 128), F32),...  7.86 us

profile of v1, /device:TPU:42, one launch (start us, length us, event | category | flops | bytes accessed | tf_op | source)
XLA Modules:
  0.0 247.3 jit_solution(11842976669627968359)
XLA Ops:
  0.0 0.8 dynamic_slice.6
  0.8 0.8 dynamic_slice.7
  1.5 0.6 pad_maximum_fusion.gains
  2.1 94.7 %spread.1 = (bf16[16,112,448]{2,1,0:T(8,128)(2,1)}, bf16[112,448]{1,0:T(8,128)(2,1)}, bf16[2,3,448,384]{3,2,1,0:T(8,128)(2,1)}, bf16[2,448,384]{2,1,0:T(8,128)(2...) custom-call(bf16[98,448]{1,0:T(8,128)(2,1)} %tok.3, f32[2,448]{1,0:T(2,128)} %pad_maximum_fusion.gains, ...), custom_call_target="tpu_custom_call" | custom-call | tf_op jit(solution)/shard_map/spread/pallas_call | solution.py:225
  96.9 7.9 %project.1 = (f32[8,9,112,128]{3,2,1,0:T(8,128)}, f32[32,128]{1,0:T(8,128)}) custom-call(s32[1,5]{1,0:T(1,128)} %table.3, bf16[16,112,448]{2,1,0:T(8,128)(2,1)} %get-tuple-element.15.gathered, bf16[112,448]{1,0:T(8,128)(2,1)} %get-tuple-element.16.normed, bf16[2,3,448,384]{3,2,1,0:T(8,128)(2,1)} %get-tuple-element.17.w_both, ...), custom_call_target="tpu_custom_call" | custom-call | tf_op jit(solution)/shard_map/project/pallas_call | solution.py:288
  104.7 44.0 %reduce.1 = (f32[9,112,128]{2,1,0:T(8,128)}, f32[16,32,128]{2,1,0:T(8,128)}) custom-call(f32[8,9,112,128]{3,2,1,0:T(8,128)} %get-tuple-element.19.part, f32[32,128]{1,0:T(8,128)} %get-tuple-element.20.low), custom_call_target="tpu_custom_call" | custom-call | tf_op jit(solution)/shard_map/reduce/pallas_call | solution.py:360
  148.8 0.0 copy-start
  148.8 13.7 %reshape.7.cache = bf16[2,4096,384]{2,1,0:T(8,128)(2,1)} reshape(bf16[2,2048,2,384]{3,2,1,0:T(2,128)(2,1)} %param.22) | data formatting | bytes 12582912 | tf_op jit(solution)/shard_map/reshape | solution.py:609
  162.5 0.0 copy-done
  162.5 0.6 reshape.6.bias
  163.2 8.4 %attend.1.att = bf16[112,384]{1,0:T(8,128)(2,1)} custom-call(s32[1,5]{1,0:T(1,128)} %table.3, s32[3]{0:T(128)} %lengths.1, s32[2]{0:T(128)} %cache_lengths.1, f32[9,112,128]{2,1,0:T(8,128)} %get-tuple-element.21.sums, f32[16,32,128]{2,1,0:T(8,128)} %get-tuple-element.22.lows, bf16[2,8,4,2,16,384]{5,4,3,2,1,0:T(8,128)(2,1)} %get-tuple-element.23.up_all, ...), custom_call_target="tpu_custom_call" | custom-call | tf_op jit(solution)/shard_map/attend/pallas_call | solution.py:452
  171.5 17.9 %collect.1.every = bf16[8,112,384]{2,1,0:T(8,128)(2,1)} custom-call(bf16[112,384]{1,0:T(8,128)(2,1)} %attend.1.att), custom_call_target="tpu_custom_call" | custom-call | tf_op jit(solution)/shard_map/collect/pallas_call | solution.py:483
  189.4 3.7 %mix.1.pieces = bf16[16,112,448]{2,1,0:T(8,128)(2,1)} custom-call(bf16[8,112,384]{2,1,0:T(8,128)(2,1)} %collect.1.every, bf16[2,448,384]{2,1,0:T(8,128)(2,1)} %get-tuple-element.24.wo_both), custom_call_target="tpu_custom_call" | custom-call | tf_op jit(solution)/shard_map/mix/pallas_call | solution.py:504
  193.1 52.6 %scatter.1 = bf16[98,448]{1,0:T(8,128)(2,1)} custom-call(bf16[16,112,448]{2,1,0:T(8,128)(2,1)} %mix.1.pieces, bf16[98,448]{1,0:T(8,128)(2,1)} %tok.3, f32[1,448]{1,0:T(1,128)} %bitcast.9), custom_call_target="tpu_custom_call" | custom-call | tf_op jit(solution)/shard_map/scatter/pallas_call | solution.py:564
  245.7 1.5 copy.15
Async XLA Ops:
  148.8 13.8 %copy-start = (f32[3,384]{1,0:T(4,128)S(1)}, f32[3,384]{1,0:T(4,128)}, u32[]{:S(2)}) copy-start(f32[3,384]{1,0:T(4,128)} %param.17) | copy-start | bytes 13828
